TPU v7x, 128 devices: a whole 4x4x4 slice. The times are simulated.
128 devices in a mesh: outer: 2 (over core), inner: 64 (over y, x, z).
Axes of the slice: x: 4, y: 4, z: 4, core: 2. Of those that a mesh axis runs over, the one named last changes fastest.
Arguments:
- features: float32 [262144, 1024], P(('outer', 'inner'))
- dest: int32 [8192], P(('outer', 'inner')), may hold values from 0 to 63, as said below
- slot: int32 [8192], P(('outer', 'inner')), may hold values from 0 to 63, as said below
Outputs:
- standardized: float32 [262144, 1024], P(('outer', 'inner'))
- moments: float32 [2, 1024], replicated
Inputs may be any that keep to these rules, and one draw needn't show every extreme that they name: `dest`: blocks of one device name destinations in the same shuffle domain; from one device at most 1 block go to any one destination, and exactly 1 to each destination it names. Every device of a shuffle domain receives exactly 64 blocks, each with a different slot.
All inputs are finite; a program needn't handle non-finite values.
Results may differ from a plain program's by a relative error of at most 0.000031.
Values sent between devices are 32-bit elements; how exact they have to be, the bound alone decides.
A program may use at most 128 MiB of HBM per device.

v0:
```python
import jax
import jax.numpy as jnp
from jax import lax
from jax.sharding import PartitionSpec as P

eps_value = 1e-06
clip_value = 3.0


def partner(array, axis, stride):
    return lax.ppermute(array, axis, [(i, i ^ 1 << stride) for i in range(lax.axis_size(axis))])


def merge_pair(center_a, spread_a, center_b, spread_b, half):
    gap = center_b - center_a
    return ((center_a + center_b) * 0.5, spread_a + spread_b + gap * gap * half)


def standardize(block_rows, center, factor):
    return jnp.clip((block_rows - center) * factor, -clip_value, clip_value)


def body(features, dest, slot):
    row_count, feat_width = features.shape
    block_count = dest.shape[0]
    block_rows = row_count // block_count
    peer_count = lax.axis_size("inner")
    outer_count = lax.axis_size("outer")
    capacity = max(1, block_count // peer_count)
    total_rows = row_count * peer_count * outer_count
    local_center = jnp.mean(features, axis=0)
    deviation = features - local_center
    local_spread = jnp.sum(deviation * deviation, axis=0)
    center, spread = (local_center, local_spread)
    level_count = row_count
    for bit_index in range(peer_count.bit_length() - 1):
        other_center, other_spread = partner((center, spread), "inner", bit_index)
        center, spread = merge_pair(center, spread, other_center, other_spread, level_count * 0.5)
        level_count = level_count * 2
    bit_index = 0
    other_center, other_spread = partner((center, spread), "outer", bit_index)
    center, spread = merge_pair(center, spread, other_center, other_spread, level_count * 0.5)
    variance = spread / total_rows
    factor = lax.rsqrt(variance + eps_value)
    peer_ids = jnp.arange(peer_count, dtype=jnp.int32)
    hits = (dest[:, None] == peer_ids[None, :]).astype(jnp.int32)
    earlier = jnp.cumsum(hits, axis=0) - hits
    within = jnp.sum(earlier * hits, axis=1)
    target_cell = dest * capacity + within
    cell_ids = jnp.arange(peer_count * capacity, dtype=jnp.int32)
    matches = target_cell[:, None] == cell_ids[None, :]
    block_ids = jnp.arange(block_count, dtype=jnp.int32)
    source_block = jnp.sum(jnp.where(matches, block_ids[:, None], 0), axis=0)
    occupied = jnp.any(matches, axis=0)
    sent_slot = jnp.where(occupied, slot[source_block], -1).reshape(peer_count, capacity)
    blocks = features.reshape(block_count, block_rows, feat_width)
    picked = jnp.where(occupied[:, None, None], blocks[source_block], 0.0)
    received = lax.all_to_all(
        picked.reshape(peer_count, capacity, block_rows, feat_width),
        "inner",
        split_axis=0,
        concat_axis=0,
        tiled=True,
    )
    got_slot = lax.all_to_all(sent_slot, "inner", split_axis=0, concat_axis=0, tiled=True)
    flat_blocks = received.reshape(peer_count * capacity, block_rows, feat_width)
    slot_hits = got_slot.reshape(-1)[:, None] == block_ids[None, :]
    chosen = jnp.sum(jnp.where(slot_hits, cell_ids[:, None], 0), axis=0)
    standardized = standardize(flat_blocks[chosen].reshape(row_count, feat_width), center, factor)
    return (standardized, jnp.stack([center, variance]))


def solution(mesh):
    in_specs = (P(("outer", "inner"), None), P(("outer", "inner")), P(("outer", "inner")))
    out_specs = (P(("outer", "inner"), None), P())
    return jax.shard_map(body, mesh=mesh, in_specs=in_specs, out_specs=out_specs, check_vma=False)
```

profile of v0, /device:TPU:1, one launch (start us, length us, event | category | flops | bytes accessed | tf_op | source)
XLA Modules:
  0.0 197.7 jit_solution(9059658725770701739)
XLA Ops:
  0.6 0.0 copy-start
  0.6 0.7 fusion.3
  1.4 0.1 reduce_window_sum.11
  1.5 0.8 select_reduce_fusion.2
  2.3 0.7 add.93
  3.0 0.1 select_reduce_fusion.1
  3.1 0.1 fusion.2
  3.2 0.0 copy-done
  3.2 0.8 gather_fusion.1
  4.0 0.7 copy.6
  4.7 12.0 %all-to-all-start.1 = ((s32[64,1,1]{2,1,0:T(1,128)}), s32[64,1,1]{2,1,0:T(1,128)S(1)}, u32[]{:S(2)}, u32[]{:S(2)}) async-start(s32[64,1,1]{2,1,0:T(1,128)} %copy.6), calls=%async_computation.1 | async-start | bytes 65536 | tf_op jit(solution)/shard_map/all_to_all | solution.py:65
  16.7 7.9 %gather_fusion = f32[64,32,1024]{2,1,0:T(8,128)} fusion(f32[64,32,1024]{2,1,0:T(8,128)} %bitcast.22, s32[1024]{0:T(1024)S(1)} %pad_clamp_fusion.1), kind=kCustom, calls=%fused_computation | custom fusion | bytes 16777472 | tf_op jit(solution)/shard_map/gather | solution.py:57
  24.5 8.7 %bitcast_select_fusion = f32[64,1,32,1024]{3,2,1,0:T(8,128)} fusion(f32[64,32,1024]{2,1,0:T(8,128)} %gather_fusion, pred[64]{0:T(512)(128)(4,1)S(1)} %fusion.2), kind=kLoop, calls=%fused_computation.6 | loop fusion | flops 2097152 | bytes 16777280 | tf_op jit(solution)/shard_map/jit(_where)/select_n | solution.py:57
  33.2 0.0 all-to-all-done.1
  33.3 10.0 %all-to-all-start = ((f32[64,1,32,1024]{3,2,1,0:T(8,128)}), f32[64,1,32,1024]{3,2,1,0:T(8,128)}, u32[]{:S(2)}, u32[]{:S(2)}) async-start(f32[64,1,32,1024]{3,2,1,0:T(8,128)} %bitcast_select_fusion), calls=%async_computation | async-start | bytes 16777216 | tf_op jit(solution)/shard_map/all_to_all | solution.py:58
  43.3 3.9 %reduce_sum.54 = f32[1024]{0:T(1024)S(1)} reduce(f32[2048,1024]{1,0:T(8,128)} %param.3, f32[]{:T(128)} %constant.8.clone.1), dimensions={0}, to_apply=%region_5.6 | reduce | flops 2096128 | bytes 8392708 | tf_op jit(solution)/shard_map/reduce_sum | solution.py:31
  47.2 1.0 collective-permute-start
  48.2 4.3 %multiply_reduce_fusion = f32[1024]{0:T(1024)S(1)} fusion(f32[2048,1024]{1,0:T(8,128)} %param.3, f32[1024]{0:T(1024)S(1)} %broadcast_multiply_fusion), kind=kLoop, calls=%fused_computation.7 | loop fusion | flops 6290432 | bytes 8396800 | tf_op jit(solution)/shard_map/reduce_sum | solution.py:33
  52.5 0.6 collective-permute-start.7
  53.1 15.0 %collective-permute-done = f32[1024]{0:T(1024)S(1)} collective-permute-done((f32[1024]{0:T(1024)S(1)}, f32[1024]{0:T(1024)S(1)}, u32[]{:S(2)}, u32[]{:S(2)}) %collective-permute-start) | collective-permute-done | bytes 4128 | tf_op jit(solution)/shard_map/ppermute | solution.py:11
  68.1 0.4 collective-permute-done.7
  68.5 28.6 %collective-permute-start.1 = (f32[1024]{0:T(1024)S(1)}, f32[1024]{0:T(1024)S(1)}, u32[]{:S(2)}, u32[]{:S(2)}) collective-permute-start(f32[1024]{0:T(1024)S(1)} %get-tuple-element.16), channel_id=1, source_target_pairs={{0,2},{1,3},{2,0},{3,1},{4,6},{5,7},{6,4},{7,5},{8,10},{9,11},{10,... | collective-permute-start | bytes 12296 | tf_op jit(solution)/shard_map/ppermute | solution.py:11
  97.1 0.1 collective-permute-start.8
  97.2 1.4 collective-permute-done.1
  98.6 4.8 %collective-permute-done.8 = f32[1024]{0:T(1024)S(1)} collective-permute-done((f32[1024]{0:T(1024)S(1)}, f32[1024]{0:T(1024)S(1)}, u32[]{:S(2)}, u32[]{:S(2)}) %collective-permute-start.8) | collective-permute-done | bytes 4128 | tf_op jit(solution)/shard_map/ppermute | solution.py:11
  103.4 0.0 collective-permute-start.2
  103.4 1.5 collective-permute-start.9
  104.8 49.3 %collective-permute-done.2 = f32[1024]{0:T(1024)S(1)} collective-permute-done((f32[1024]{0:T(1024)S(1)}, f32[1024]{0:T(1024)S(1)}, u32[]{:S(2)}, u32[]{:S(2)}) %collective-permute-start.2) | collective-permute-done | bytes 4128 | tf_op jit(solution)/shard_map/ppermute | solution.py:11
  154.2 0.1 collective-permute-done.9
  154.2 4.0 %collective-permute-start.3 = (f32[1024]{0:T(1024)S(1)}, f32[1024]{0:T(1024)S(1)}, u32[]{:S(2)}, u32[]{:S(2)}) collective-permute-start(f32[1024]{0:T(1024)S(1)} %get-tuple-element.12), channel_id=1, source_target_pairs={{0,8},{1,9},{2,10},{3,11},{4,12},{5,13},{6,14},{7,15},{8,0},{9,1},... | collective-permute-start | bytes 12296 | tf_op jit(solution)/shard_map/ppermute | solution.py:11
  158.2 0.1 collective-permute-start.10
  158.3 1.2 reduce
  159.5 0.0 collective-permute-done.3
  159.5 2.9 %collective-permute-done.10 = f32[1024]{0:T(1024)S(1)} collective-permute-done((f32[1024]{0:T(1024)S(1)}, f32[1024]{0:T(1024)S(1)}, u32[]{:S(2)}, u32[]{:S(2)}) %collective-permute-start.10) | collective-permute-done | bytes 4128 | tf_op jit(solution)/shard_map/ppermute | solution.py:11
  162.5 0.1 collective-permute-start.4
  162.6 1.3 collective-permute-start.11
  163.9 0.1 select_reduce_fusion
  164.0 1.2 collective-permute-done.4
  165.2 0.1 collective-permute-done.11
  165.3 4.0 %collective-permute-start.5 = (f32[1024]{0:T(1024)S(1)}, f32[1024]{0:T(1024)S(1)}, u32[]{:S(2)}, u32[]{:S(2)}) collective-permute-start(f32[1024]{0:T(1024)S(1)} %get-tuple-element.8), channel_id=1, source_target_pairs={{0,32},{1,33},{2,34},{3,35},{4,36},{5,37},{6,38},{7,39},{8,40},{9,... | collective-permute-start | bytes 12296 | tf_op jit(solution)/shard_map/ppermute | solution.py:11
  169.3 0.1 collective-permute-start.12
  169.4 0.9 collective-permute-done.5
  170.3 3.0 %collective-permute-done.12 = f32[1024]{0:T(1024)S(1)} collective-permute-done((f32[1024]{0:T(1024)S(1)}, f32[1024]{0:T(1024)S(1)}, u32[]{:S(2)}, u32[]{:S(2)}) %collective-permute-start.12) | collective-permute-done | bytes 4128 | tf_op jit(solution)/shard_map/ppermute | solution.py:11
  173.3 6.1 %collective-permute-start.6 = (f32[1024]{0:T(1024)S(1)}, f32[1024]{0:T(1024)S(1)}, u32[]{:S(2)}, u32[]{:S(2)}) collective-permute-start(f32[1024]{0:T(1024)S(1)} %get-tuple-element.6), channel_id=1, source_target_pairs={{0,64},{64,0},{1,65},{65,1},{2,66},{66,2},{3,67},{67,3},{4,68},{68... | collective-permute-start | bytes 12296 | tf_op jit(solution)/shard_map/ppermute | solution.py:11
  179.4 0.1 collective-permute-start.13
  179.5 0.7 collective-permute-done.6
  180.2 0.3 collective-permute-done.13
  180.6 0.6 pad_maximum_fusion
  181.2 0.0 all-to-all-done
  181.2 7.7 %gather_fusion.2 = f32[64,32,1024]{2,1,0:T(8,128)} fusion(f32[64,32,1024]{2,1,0:T(8,128)} %bitcast.4, s32[1024]{0:T(1024)S(1)} %pad_clamp_fusion), kind=kCustom, calls=%fused_computation.2 | custom fusion | bytes 16777472 | tf_op jit(solution)/shard_map/gather | solution.py:69
  188.9 8.8 %fusion.1 = f32[2048,1024]{1,0:T(8,128)} fusion(f32[64,32,1024]{2,1,0:T(8,128)} %gather_fusion.2, f32[1024]{0:T(1024)S(1)} %get-tuple-element.2, f32[1024]{0:T(1024)S(1)} %get-tuple-element.4), kind=kLoop, calls=%fused_computation.5 | loop fusion | flops 6291456 | bytes 16785408 | tf_op jit(solution)/shard_map/jit(clip)/min | solution.py:20
  (13 shorter events, 0.1 us)
Async XLA Ops:
  0.6 2.6 %copy-start = (s32[64]{0:T(128)S(1)}, s32[64]{0:T(128)}, u32[]{:S(2)}) copy-start(s32[64]{0:T(128)} %param.5) | copy-start | bytes 772
  4.7 28.6 %all-to-all-start.1 = ((s32[64,1,1]{2,1,0:T(1,128)}), s32[64,1,1]{2,1,0:T(1,128)S(1)}, u32[]{:S(2)}, u32[]{:S(2)}) async-start(s32[64,1,1]{2,1,0:T(1,128)} %copy.6), calls=%async_computation.1 | async-start | bytes 65536 | tf_op jit(solution)/shard_map/all_to_all | solution.py:65
  33.3 148.0 %all-to-all-start = ((f32[64,1,32,1024]{3,2,1,0:T(8,128)}), f32[64,1,32,1024]{3,2,1,0:T(8,128)}, u32[]{:S(2)}, u32[]{:S(2)}) async-start(f32[64,1,32,1024]{3,2,1,0:T(8,128)} %bitcast_select_fusion), calls=%async_computation | async-start | bytes 16777216 | tf_op jit(solution)/shard_map/all_to_all | solution.py:58
  47.2 20.9 %collective-permute-start = (f32[1024]{0:T(1024)S(1)}, f32[1024]{0:T(1024)S(1)}, u32[]{:S(2)}, u32[]{:S(2)}) collective-permute-start(f32[1024]{0:T(1024)S(1)} %broadcast_multiply_fusion), channel_id=1, source_target_pairs={{0,1},{1,0},{2,3},{3,2},{4,5},{5,4},{6,7},{7,6},{8,9},{9,8},{10,11... | collective-permute-start | bytes 12296 | tf_op jit(solution)/shard_map/ppermute | solution.py:11
  52.5 16.0 %collective-permute-start.7 = (f32[1024]{0:T(1024)S(1)}, f32[1024]{0:T(1024)S(1)}, u32[]{:S(2)}, u32[]{:S(2)}) collective-permute-start(f32[1024]{0:T(1024)S(1)} %multiply_reduce_fusion), channel_id=1, source_target_pairs={{0,1},{1,0},{2,3},{3,2},{4,5},{5,4},{6,7},{7,6},{8,9},{9,8},{10,11... | collective-permute-start | bytes 12296 | tf_op jit(solution)/shard_map/ppermute | solution.py:11
  68.5 30.1 %collective-permute-start.1 = (f32[1024]{0:T(1024)S(1)}, f32[1024]{0:T(1024)S(1)}, u32[]{:S(2)}, u32[]{:S(2)}) collective-permute-start(f32[1024]{0:T(1024)S(1)} %get-tuple-element.16), channel_id=1, source_target_pairs={{0,2},{1,3},{2,0},{3,1},{4,6},{5,7},{6,4},{7,5},{8,10},{9,11},{10,... | collective-permute-start | bytes 12296 | tf_op jit(solution)/shard_map/ppermute | solution.py:11
  97.1 6.3 %collective-permute-start.8 = (f32[1024]{0:T(1024)S(1)}, f32[1024]{0:T(1024)S(1)}, u32[]{:S(2)}, u32[]{:S(2)}) collective-permute-start(f32[1024]{0:T(1024)S(1)} %get-tuple-element.15), channel_id=1, source_target_pairs={{0,2},{1,3},{2,0},{3,1},{4,6},{5,7},{6,4},{7,5},{8,10},{9,11},{10,... | collective-permute-start | bytes 12296 | tf_op jit(solution)/shard_map/ppermute | solution.py:11
  103.4 50.8 %collective-permute-start.2 = (f32[1024]{0:T(1024)S(1)}, f32[1024]{0:T(1024)S(1)}, u32[]{:S(2)}, u32[]{:S(2)}) collective-permute-start(f32[1024]{0:T(1024)S(1)} %get-tuple-element.14), channel_id=1, source_target_pairs={{0,4},{1,5},{2,6},{3,7},{4,0},{5,1},{6,2},{7,3},{8,12},{9,13},{10,... | collective-permute-start | bytes 12296 | tf_op jit(solution)/shard_map/ppermute | solution.py:11
  103.4 50.8 %collective-permute-start.9 = (f32[1024]{0:T(1024)S(1)}, f32[1024]{0:T(1024)S(1)}, u32[]{:S(2)}, u32[]{:S(2)}) collective-permute-start(f32[1024]{0:T(1024)S(1)} %get-tuple-element.13), channel_id=1, source_target_pairs={{0,4},{1,5},{2,6},{3,7},{4,0},{5,1},{6,2},{7,3},{8,12},{9,13},{10,... | collective-permute-start | bytes 12296 | tf_op jit(solution)/shard_map/ppermute | solution.py:11
  154.2 5.3 %collective-permute-start.3 = (f32[1024]{0:T(1024)S(1)}, f32[1024]{0:T(1024)S(1)}, u32[]{:S(2)}, u32[]{:S(2)}) collective-permute-start(f32[1024]{0:T(1024)S(1)} %get-tuple-element.12), channel_id=1, source_target_pairs={{0,8},{1,9},{2,10},{3,11},{4,12},{5,13},{6,14},{7,15},{8,0},{9,1},... | collective-permute-start | bytes 12296 | tf_op jit(solution)/shard_map/ppermute | solution.py:11
  158.2 4.2 %collective-permute-start.10 = (f32[1024]{0:T(1024)S(1)}, f32[1024]{0:T(1024)S(1)}, u32[]{:S(2)}, u32[]{:S(2)}) collective-permute-start(f32[1024]{0:T(1024)S(1)} %get-tuple-element.11), channel_id=1, source_target_pairs={{0,8},{1,9},{2,10},{3,11},{4,12},{5,13},{6,14},{7,15},{8,0},{9,1},... | collective-permute-start | bytes 12296 | tf_op jit(solution)/shard_map/ppermute | solution.py:11
  162.5 2.8 %collective-permute-start.4 = (f32[1024]{0:T(1024)S(1)}, f32[1024]{0:T(1024)S(1)}, u32[]{:S(2)}, u32[]{:S(2)}) collective-permute-start(f32[1024]{0:T(1024)S(1)} %get-tuple-element.10), channel_id=1, source_target_pairs={{0,16},{1,17},{2,18},{3,19},{4,20},{5,21},{6,22},{7,23},{8,24},{9,... | collective-permute-start | bytes 12296 | tf_op jit(solution)/shard_map/ppermute | solution.py:11
  162.6 2.8 %collective-permute-start.11 = (f32[1024]{0:T(1024)S(1)}, f32[1024]{0:T(1024)S(1)}, u32[]{:S(2)}, u32[]{:S(2)}) collective-permute-start(f32[1024]{0:T(1024)S(1)} %get-tuple-element.9), channel_id=1, source_target_pairs={{0,16},{1,17},{2,18},{3,19},{4,20},{5,21},{6,22},{7,23},{8,24},{9,... | collective-permute-start | bytes 12296 | tf_op jit(solution)/shard_map/ppermute | solution.py:11
  165.3 5.0 %collective-permute-start.5 = (f32[1024]{0:T(1024)S(1)}, f32[1024]{0:T(1024)S(1)}, u32[]{:S(2)}, u32[]{:S(2)}) collective-permute-start(f32[1024]{0:T(1024)S(1)} %get-tuple-element.8), channel_id=1, source_target_pairs={{0,32},{1,33},{2,34},{3,35},{4,36},{5,37},{6,38},{7,39},{8,40},{9,... | collective-permute-start | bytes 12296 | tf_op jit(solution)/shard_map/ppermute | solution.py:11
  169.3 4.0 %collective-permute-start.12 = (f32[1024]{0:T(1024)S(1)}, f32[1024]{0:T(1024)S(1)}, u32[]{:S(2)}, u32[]{:S(2)}) collective-permute-start(f32[1024]{0:T(1024)S(1)} %get-tuple-element.7), channel_id=1, source_target_pairs={{0,32},{1,33},{2,34},{3,35},{4,36},{5,37},{6,38},{7,39},{8,40},{9,... | collective-permute-start | bytes 12296 | tf_op jit(solution)/shard_map/ppermute | solution.py:11
  173.3 6.9 %collective-permute-start.6 = (f32[1024]{0:T(1024)S(1)}, f32[1024]{0:T(1024)S(1)}, u32[]{:S(2)}, u32[]{:S(2)}) collective-permute-start(f32[1024]{0:T(1024)S(1)} %get-tuple-element.6), channel_id=1, source_target_pairs={{0,64},{64,0},{1,65},{65,1},{2,66},{66,2},{3,67},{67,3},{4,68},{68... | collective-permute-start | bytes 12296 | tf_op jit(solution)/shard_map/ppermute | solution.py:11
  179.4 1.2 collective-permute-start.13
where the time goes:
time: 198 us
  waiting for transfers between devices  80.1 us (40%)
  starting transfers between devices  69.6 us (35%)
  other arithmetic  30.3 us (15%)
  local copies, waits for them, and re-layouts  17.1 us (9%)
    ppermute x14, waiting for transfers between devices, partner(): lax.ppermute(array, axis, [(i, i ^ 1 << stride) for i in range(lax.axis_s...  80.1 us
    ppermute x14, starting transfers between devices, partner(): lax.ppermute(array, axis, [(i, i ^ 1 << stride) for i in range(lax.axis_s...  47.6 us
    all_to_all x1, starting transfers between devices, body(): lax.all_to_all(sent_slot, 'inner', split_axis=0, concat_axis=0, tiled=True)  12 us
    all_to_all x1, starting transfers between devices, body(): lax.all_to_all(picked.reshape(peer_count, capacity, block_rows, feat_widt...  10 us
    min x1, other arithmetic, standardize(): return jnp.clip((block_rows - center) * factor, -clip_value, clip_value)  8.82 us
    select_n x2, other arithmetic, body(): picked = jnp.where(occupied[:, None, None], blocks[source_block], 0.0)  8.72 us
    gather x1, local copies, waits for them, and re-layouts, body(): picked = jnp.where(occupied[:, None, None], blocks[source_block], 0.0)  7.86 us
    gather x1, local copies, waits for them, and re-layouts, body(): flat_blocks[chosen].reshape(row_count, feat_width)  7.69 us
  transfers between devices with their start and end apart: 16, of which 13 were waited for; matrix products, arithmetic and copies ran while one was open for 14% of the time, Pallas kernels for 0%

commit v1 on v0

v1 whole, which is shorter than its diff:
```python
import functools
import itertools

import jax
import jax.numpy as jnp
from jax import lax
from jax.experimental import pallas as pl
from jax.experimental.pallas import tpu as pltpu
from jax.sharding import PartitionSpec as P

MESH = pl.DeviceIdType.MESH
eps_value = 1e-06
clip_value = 3.0
SIDE = 4
PIECES = 8
WINDOW = 21
LOADS = 8
LANES = 128


def hops(offset):
    return sum(min(v, SIDE - v) for v in offset)


def send_order():
    left = [d for d in itertools.product(range(SIDE), repeat=3) if any(d)]
    groups = []
    while left:
        first, group = left[0], []
        for shift in range(3):
            for sign in (1, -1):
                d = tuple(sign * first[(j + shift) % 3] % SIDE for j in range(3))
                if d in left:
                    left.remove(d)
                    group.append(d)
        groups.append(group)
    return [d for group in sorted(groups, key=lambda g: hops(g[0])) for d in group]


def merge_pair(a, b, half):
    gap = b[0] - a[0]
    return ((a[0] + b[0]) * 0.5, a[1] + b[1] + gap * gap * half)


def exchange_kernel(
    dest_ref, slot_ref, feat_hbm,
    land_ref, slots_ref, stat_ref,
    feats, stage, order_v, slot_v, order_s, moment, peer_moment,
    load_sem, order_sem, send_sem, land_sem, slot_send, slot_recv, mom_send, mom_recv,
):
    peers, rows, width = land_ref.shape
    tiles = width // LANES
    piece = rows // PIECES if rows // PIECES >= 8 else 8
    row_pieces = rows // piece
    col_pieces = PIECES // row_pieces
    cols = width // col_pieces
    core, me = lax.axis_index("outer"), lax.axis_index("inner")
    y, x, z = me // (SIDE * SIDE), (me // SIDE) % SIDE, me % SIDE

    def at(offset):
        dy, dx, dz = offset
        return ((y + dy) % SIDE) * SIDE * SIDE + ((x + dx) % SIDE) * SIDE + (z + dz) % SIDE

    barrier = pltpu.get_barrier_semaphore()

    def greet(k, carry):
        pl.semaphore_signal(barrier, inc=1, device_id=(core, me ^ k), device_id_type=MESH)
        return carry

    lax.fori_loop(1, peers, greet, 0)
    pl.semaphore_signal(barrier, inc=1, device_id=(1 - core, me), device_id_type=MESH)

    load = peers // LOADS
    loads = [
        pltpu.make_async_copy(
            feat_hbm.at[pl.ds(k * load, load)], feats.at[pl.ds(k * load, load)], load_sem.at[k]
        )
        for k in range(LOADS)
    ]
    for copy in loads:
        copy.start()

    blocks = dest_ref.shape[1]
    hit = dest_ref[...] == lax.broadcasted_iota(jnp.int32, (peers, blocks), 0)
    ids = lax.broadcasted_iota(jnp.int32, (peers, blocks), 1)
    order = jnp.max(jnp.where(hit, ids, 0), axis=1, keepdims=True)
    slots = jnp.max(jnp.where(hit, slot_ref[...], 0), axis=1, keepdims=True)
    order_v[...] = jnp.broadcast_to(order, order_v.shape)
    slot_v[...] = jnp.broadcast_to(slots, slot_v.shape)
    to_scalar = pltpu.make_async_copy(order_v, order_s, order_sem)
    to_scalar.start()
    to_scalar.wait()
    for copy in loads:
        copy.wait()

    def arrange(p, carry):
        stage[p] = feats[order_s[p, 0]]
        return carry

    lax.fori_loop(0, peers, arrange, 0)
    land_ref[me] = feats[order_s[me, 0]]
    slots_ref[pl.ds(me, 1)] = slot_v[pl.ds(me, 1)]

    pl.semaphore_wait(barrier, peers)

    def local_moments():
        def total(b, acc):
            block = feats[b]
            for r in range(0, rows, 8):
                acc = acc + block[r : r + 8]
            return acc

        zero = jnp.zeros((8, width), jnp.float32)
        count = peers * rows
        center = jnp.sum(lax.fori_loop(0, peers, total, zero), axis=0, keepdims=True) * (1.0 / count)
        wide = jnp.broadcast_to(center, (8, width))

        def squares(b, acc):
            block = feats[b]
            for r in range(0, rows, 8):
                gap = block[r : r + 8] - wide
                acc = acc + gap * gap
            return acc

        spread = jnp.sum(lax.fori_loop(0, peers, squares, zero), axis=0, keepdims=True)
        for t in range(tiles):
            moment[0, pl.ds(t, 1)] = center[:, t * LANES : (t + 1) * LANES]
            moment[0, pl.ds(tiles + t, 1)] = spread[:, t * LANES : (t + 1) * LANES]

    def read(ref):
        return ref[pl.ds(0, tiles)], ref[pl.ds(tiles, tiles)]

    def write(ref, pair):
        ref[pl.ds(0, tiles)] = pair[0]
        ref[pl.ds(tiles, tiles)] = pair[1]

    def moment_copies(step):
        if step == 3:
            targets = [(1 - core, me)]
        else:
            targets = [(core, me ^ (k * SIDE**step)) for k in (1, 2, 3)]
        return [
            pltpu.make_async_remote_copy(
                src_ref=moment.at[step],
                dst_ref=peer_moment.at[step * 3 + k],
                send_sem=mom_send.at[step * 3 + k],
                recv_sem=mom_recv.at[step * 3 + k],
                device_id=target,
                device_id_type=MESH,
            )
            for k, target in enumerate(targets)
        ]

    def moment_send(step):
        for copy in moment_copies(step):
            copy.start()

    def moment_merge(step):
        for copy in moment_copies(step):
            copy.wait()
        count = float(peers * rows * SIDE**step)
        pair = merge_pair(read(moment.at[step]), read(peer_moment.at[step * 3]), count * 0.5)
        if step < 3:
            other = merge_pair(
                read(peer_moment.at[step * 3 + 1]), read(peer_moment.at[step * 3 + 2]), count * 0.5
            )
            pair = merge_pair(pair, other, count)
            write(moment.at[step + 1], pair)
            moment_send(step + 1)
        else:
            write(stat_ref, (pair[0], pair[1] / (count * 2.0)))

    targets = [at(d) for d in send_order()]

    def slot_copy(j):
        return pltpu.make_async_remote_copy(
            src_ref=slot_v.at[pl.ds(targets[j], 1)],
            dst_ref=slots_ref.at[pl.ds(me, 1)],
            send_sem=slot_send.at[j],
            recv_sem=slot_recv,
            device_id=(core, targets[j]),
            device_id_type=MESH,
        )

    def piece_copy(q, j):
        part = (pl.ds((q // col_pieces) * piece, piece), pl.ds(pl.multiple_of((q % col_pieces) * cols, cols), cols))
        return pltpu.make_async_remote_copy(
            src_ref=stage.at[(targets[j],) + part],
            dst_ref=land_ref.at[(me,) + part],
            send_sem=send_sem.at[j % WINDOW],
            recv_sem=land_sem,
            device_id=(core, targets[j]),
            device_id_type=MESH,
        )

    def run(q, carry):
        for j in range(peers - 1):
            if j < WINDOW:

                @pl.when(q > 0)
                def _():
                    piece_copy(q, j).wait_send()
            else:
                piece_copy(q, j).wait_send()
            piece_copy(q, j).start()
            if j == WINDOW - 1:

                @pl.when(q == 0)
                def _():
                    local_moments()
                    moment_send(0)
                    for i in range(peers - 1):
                        slot_copy(i).start()

        for step in range(4):

            @pl.when(q == step + 1)
            def _():
                moment_merge(step)

        return carry

    lax.fori_loop(0, PIECES, run, 0)
    for j in range(WINDOW):
        piece_copy(0, j).wait_send()
    for j in range(peers - 1):
        slot_copy(j).wait_send()
    others = pl.ds(0, peers - 1)
    pltpu.make_async_copy(slots_ref.at[others], slots_ref.at[others], slot_recv).wait()
    pltpu.make_async_copy(land_ref.at[others], land_ref.at[others], land_sem).wait()


def finish_kernel(land_ref, slots_ref, stat_ref, out_hbm, mom_ref, ready, out_sem):
    peers, rows, width = land_ref.shape
    tiles = width // LANES
    row = lambda ref, first: jnp.concatenate([ref[pl.ds(first + t, 1)] for t in range(tiles)], axis=1)
    center, variance = row(stat_ref, 0), row(stat_ref, tiles)
    mom_ref[pl.ds(0, 1)] = center
    mom_ref[pl.ds(1, 1)] = variance
    factor = lax.rsqrt(variance + eps_value)
    center = jnp.broadcast_to(center, (8, width))
    factor = jnp.broadcast_to(factor, (8, width))

    def block(s, carry):
        for r in range(0, rows, 8):
            scaled = (land_ref[s, pl.ds(r, 8)] - center) * factor
            ready[s, pl.ds(r, 8)] = jnp.clip(scaled, -clip_value, clip_value)
        pltpu.make_async_copy(ready.at[s], out_hbm.at[slots_ref[s, 0]], out_sem).start()
        return carry

    lax.fori_loop(0, peers, block, 0)
    pltpu.make_async_copy(ready, out_hbm, out_sem).wait()


def body(features, dest, slot):
    row_count, width = features.shape
    peers = lax.axis_size("inner")
    blocks = dest.shape[0]
    rows = row_count // blocks
    tiles = width // LANES
    vmem = pl.BlockSpec(memory_space=pltpu.VMEM)
    hbm = pl.BlockSpec(memory_space=pltpu.HBM)
    smem = pl.BlockSpec(memory_space=pltpu.SMEM)
    landed, slots, stats = pl.pallas_call(
        exchange_kernel,
        out_shape=[
            pltpu.VMEM((peers, rows, width), jnp.float32),
            pltpu.VMEM((peers, LANES), jnp.int32),
            pltpu.VMEM((2 * tiles, LANES), jnp.float32),
        ],
        in_specs=[vmem, vmem, hbm],
        out_specs=[vmem, vmem, vmem],
        scratch_shapes=[
            pltpu.VMEM((blocks, rows, width), jnp.float32),
            pltpu.VMEM((peers, rows, width), jnp.float32),
            pltpu.VMEM((peers, LANES), jnp.int32),
            pltpu.VMEM((peers, LANES), jnp.int32),
            pltpu.SMEM((peers, LANES), jnp.int32),
            pltpu.VMEM((4, 2 * tiles, LANES), jnp.float32),
            pltpu.VMEM((10, 2 * tiles, LANES), jnp.float32),
            pltpu.SemaphoreType.DMA((LOADS,)),
            pltpu.SemaphoreType.DMA,
            pltpu.SemaphoreType.DMA((WINDOW,)),
            pltpu.SemaphoreType.DMA,
            pltpu.SemaphoreType.DMA((peers - 1,)),
            pltpu.SemaphoreType.DMA,
            pltpu.SemaphoreType.DMA((10,)),
            pltpu.SemaphoreType.DMA((10,)),
        ],
        compiler_params=pltpu.CompilerParams(
            collective_id=0, has_side_effects=True, vmem_limit_bytes=32 * 2**20
        ),
    )(dest.reshape(1, blocks), slot.reshape(1, blocks), features.reshape(blocks, rows, width))
    standardized, moments = pl.pallas_call(
        finish_kernel,
        out_shape=[
            jax.ShapeDtypeStruct((peers, rows, width), jnp.float32),
            jax.ShapeDtypeStruct((2, width), jnp.float32),
        ],
        in_specs=[vmem, smem, vmem],
        out_specs=[hbm, vmem],
        scratch_shapes=[
            pltpu.VMEM((peers, rows, width), jnp.float32),
            pltpu.SemaphoreType.DMA,
        ],
        compiler_params=pltpu.CompilerParams(vmem_limit_bytes=24 * 2**20),
    )(landed, slots, stats)
    return (standardized.reshape(row_count, width), moments)


def solution(mesh):
    in_specs = (P(("outer", "inner"), None), P(("outer", "inner")), P(("outer", "inner")))
    out_specs = (P(("outer", "inner"), None), P())
    return jax.shard_map(body, mesh=mesh, in_specs=in_specs, out_specs=out_specs, check_vma=False)
```

time: 198 us -> 134 us (0.68)
  the two profiles are of different devices: /device:TPU:1 before, /device:TPU:92 now
where the time goes in v1:
time: 134 us
  Pallas kernels  128 us (96%)
  local copies, waits for them, and re-layouts  4.68 us (3%)
    pallas_call x1, Pallas kernels, body(): pl.pallas_call(exchange_kernel, out_shape=[pltpu.VMEM((peers, rows, width...  123 us
    pallas_call x1, Pallas kernels, body(): pl.pallas_call(finish_kernel, out_shape=[jax.ShapeDtypeStruct((peers, row...  4.94 us
    unnamed x6, local copies, waits for them, and re-layouts  4.68 us

profile of v1, /device:TPU:92, one launch (start us, length us, event | category | flops | bytes accessed | tf_op | source)
XLA Modules:
  0.0 133.7 jit_solution(14704987318694476527)
XLA Ops:
  0.6 0.0 copy-start
  0.6 3.4 %copy-done = f32[2048,1024]{1,0:T(8,128)S(1)} copy-done((f32[2048,1024]{1,0:T(8,128)S(1)}, f32[2048,1024]{1,0:T(8,128)}, u32[]{:S(2)}) %copy-start) | copy-done | bytes 8388632
  4.0 0.0 copy-start.1
  4.0 0.7 copy-done.1
  4.7 0.0 copy-start.2
  4.7 0.7 copy-done.2
  5.3 123.5 %shard_map.50 = (f32[64,32,1024]{2,1,0:T(8,128)S(1)}, s32[64,128]{1,0:T(8,128)S(1)}, f32[16,128]{1,0:T(8,128)S(1)}) custom-call(s32[1,64]{1,0:T(1,128)S(1)} %bitcast.5, s32[1,64]{1,0:T(1,128)S(1)} %bitcast.6, f32[64,32,1024]{2,1,0:T(8,128)S(1)} %bitcast.4), custom_call_target="tpu_custom_call" | custom-call | tf_op jit(solution)/shard_map/pallas_call | solution.py:264
  128.8 4.9 %shard_map.51 = (f32[64,32,1024]{2,1,0:T(8,128)}, f32[2,1024]{1,0:T(2,128)}) custom-call(f32[64,32,1024]{2,1,0:T(8,128)S(1)} %get-tuple-element.7.land_ref, s32[64,128]{1,0:T(8,128)S(1)} %get-tuple-element.8.slots_ref, f32[16,128]{1,0:T(8,128)S(1)} %get-tuple-element.9.stat_ref), custom_call_target="tpu_custom_call" | custom-call | tf_op jit(solution)/shard_map/pallas_call | solution.py:294
Async XLA Ops:
  0.6 3.4 %copy-start = (f32[2048,1024]{1,0:T(8,128)S(1)}, f32[2048,1024]{1,0:T(8,128)}, u32[]{:S(2)}) copy-start(f32[2048,1024]{1,0:T(8,128)} %param.3) | copy-start | bytes 25165828
  4.0 0.7 copy-start.1
  4.7 0.7 copy-start.2

commit v2 on v1

v2 whole, which is shorter than its diff:
```python
import itertools

import jax
import jax.numpy as jnp
from jax import lax
from jax.experimental import pallas as pl
from jax.experimental.pallas import tpu as pltpu
from jax.sharding import PartitionSpec as P

MESH = pl.DeviceIdType.MESH
eps_value = 1e-06
clip_value = 3.0
SIDE = 4
PIECES = 8
LOADS = 8
LANES = 128


def hops(offset):
    return sum(min(v, SIDE - v) for v in offset)


def send_order():
    left = [d for d in itertools.product(range(SIDE), repeat=3) if any(d)]
    groups = []
    while left:
        first, group = left[0], []
        for shift in range(3):
            for sign in (1, -1):
                d = tuple(sign * first[(j + shift) % 3] % SIDE for j in range(3))
                if d in left:
                    left.remove(d)
                    group.append(d)
        groups.append(group)
    return [d for group in sorted(groups, key=lambda g: hops(g[0])) for d in group]


def merge_pair(a, b, half):
    gap = b[0] - a[0]
    return ((a[0] + b[0]) * 0.5, a[1] + b[1] + gap * gap * half)


def exchange_kernel(
    dest_hbm, slot_hbm, feat_hbm,
    land_ref, slots_ref, stat_ref,
    feats, stage, dest_v, slot_v, order_v, slots_v, order_s, moment, peer_moment,
    load_sem, send_sem, land_sem, slot_send, slot_recv, mom_send, mom_recv,
):
    peers, rows, width = land_ref.shape
    tiles = width // LANES
    col_pieces = PIECES * 8 // rows
    cols = width // col_pieces
    core, me = lax.axis_index("outer"), lax.axis_index("inner")
    y, x, z = me // (SIDE * SIDE), (me // SIDE) % SIDE, me % SIDE

    def at(offset):
        dy, dx, dz = offset
        return ((y + dy) % SIDE) * SIDE * SIDE + ((x + dx) % SIDE) * SIDE + (z + dz) % SIDE

    barrier = pltpu.get_barrier_semaphore()
    load = peers // LOADS
    loads = [
        pltpu.make_async_copy(
            feat_hbm.at[pl.ds(k * load, load)], feats.at[pl.ds(k * load, load)], load_sem.at[k]
        )
        for k in range(LOADS)
    ]
    small = [
        pltpu.make_async_copy(dest_hbm, dest_v, load_sem.at[LOADS]),
        pltpu.make_async_copy(slot_hbm, slot_v, load_sem.at[LOADS + 1]),
    ]
    for copy in small + loads:
        copy.start()

    def greet(k, carry):
        pl.semaphore_signal(barrier, inc=1, device_id=(core, me ^ k), device_id_type=MESH)
        return carry

    lax.fori_loop(1, peers, greet, 0)
    pl.semaphore_signal(barrier, inc=1, device_id=(1 - core, me), device_id_type=MESH)

    for copy in small:
        copy.wait()
    blocks = dest_v.shape[1]
    hit = dest_v[...] == lax.broadcasted_iota(jnp.int32, (peers, blocks), 0)
    ids = lax.broadcasted_iota(jnp.int32, (peers, blocks), 1)
    order = jnp.max(jnp.where(hit, ids, 0), axis=1, keepdims=True)
    slots = jnp.max(jnp.where(hit, slot_v[...], 0), axis=1, keepdims=True)
    order_v[...] = jnp.broadcast_to(order, order_v.shape)
    slots_v[...] = jnp.broadcast_to(slots, slots_v.shape)
    to_scalar = pltpu.make_async_copy(order_v, order_s, load_sem.at[LOADS + 2])
    to_scalar.start()
    slots_ref[pl.ds(me, 1)] = slots_v[pl.ds(me, 1)]

    zero = jnp.zeros((8, width), jnp.float32)
    acc = zero
    for k in range(LOADS):
        loads[k].wait()

        def total(b, acc):
            block = feats[b]
            for r in range(0, rows, 8):
                acc = acc + block[r : r + 8]
            return acc

        acc = lax.fori_loop(k * load, (k + 1) * load, total, acc)
    center = jnp.sum(acc, axis=0, keepdims=True) * (1.0 / (peers * rows))
    to_scalar.wait()

    def part(q):
        return pl.ds((q // col_pieces) * 8, 8), pl.ds(pl.multiple_of((q % col_pieces) * cols, cols), cols)

    def arrange(q):
        def one(p, carry):
            stage[(p,) + part(q)] = feats[(order_s[p, 0],) + part(q)]
            return carry

        lax.fori_loop(0, peers, one, 0, unroll=8)

    targets = [at(d) for d in send_order()]

    def slot_copy(j):
        return pltpu.make_async_remote_copy(
            src_ref=slots_v.at[pl.ds(targets[j], 1)],
            dst_ref=slots_ref.at[pl.ds(me, 1)],
            send_sem=slot_send.at[j],
            recv_sem=slot_recv,
            device_id=(core, targets[j]),
            device_id_type=MESH,
        )

    def piece_copy(q, j):
        return pltpu.make_async_remote_copy(
            src_ref=stage.at[(targets[j],) + part(q)],
            dst_ref=land_ref.at[(me,) + part(q)],
            send_sem=send_sem.at[j],
            recv_sem=land_sem,
            device_id=(core, targets[j]),
            device_id_type=MESH,
        )

    def read(ref):
        return ref[pl.ds(0, tiles)], ref[pl.ds(tiles, tiles)]

    def write(ref, pair):
        ref[pl.ds(0, tiles)] = pair[0]
        ref[pl.ds(tiles, tiles)] = pair[1]

    def moment_copies(step):
        if step == 3:
            mates = [(1 - core, me)]
        else:
            mates = [(core, me ^ (k * SIDE**step)) for k in (1, 2, 3)]
        return [
            pltpu.make_async_remote_copy(
                src_ref=moment.at[step],
                dst_ref=peer_moment.at[step * 3 + k],
                send_sem=mom_send.at[step * 3 + k],
                recv_sem=mom_recv.at[step * 3 + k],
                device_id=mate,
                device_id_type=MESH,
            )
            for k, mate in enumerate(mates)
        ]

    def moment_send(step):
        for copy in moment_copies(step):
            copy.start()

    def moment_merge(step):
        for copy in moment_copies(step):
            copy.wait()
        count = float(peers * rows * SIDE**step)
        pair = merge_pair(read(moment.at[step]), read(peer_moment.at[step * 3]), count * 0.5)
        if step < 3:
            other = merge_pair(
                read(peer_moment.at[step * 3 + 1]), read(peer_moment.at[step * 3 + 2]), count * 0.5
            )
            pair = merge_pair(pair, other, count)
            write(moment.at[step + 1], pair)
            moment_send(step + 1)
        else:
            write(stat_ref, (pair[0], pair[1] / (count * 2.0)))

    arrange(0)
    pl.semaphore_wait(barrier, peers)
    for j in range(peers - 1):
        piece_copy(0, j).start()
    arrange(1)
    wide = jnp.broadcast_to(center, (8, width))

    def squares(b, acc):
        block = feats[b]
        for r in range(0, rows, 8):
            gap = block[r : r + 8] - wide
            acc = acc + gap * gap
        return acc

    spread = jnp.sum(lax.fori_loop(0, peers, squares, zero), axis=0, keepdims=True)
    for t in range(tiles):
        moment[0, pl.ds(t, 1)] = center[:, t * LANES : (t + 1) * LANES]
        moment[0, pl.ds(tiles + t, 1)] = spread[:, t * LANES : (t + 1) * LANES]
    moment_send(0)
    land_ref[me] = feats[order_s[me, 0]]

    def run(q, carry):
        for j in range(peers - 1):
            piece_copy(q - 1, j).wait_send()
            piece_copy(q, j).start()

            @pl.when(q == 1)
            def _():
                slot_copy(j).start()

        @pl.when(q < PIECES - 1)
        def _():
            arrange(q + 1)

        for step in range(4):

            @pl.when(q == step + 2)
            def _():
                moment_merge(step)

        return carry

    lax.fori_loop(1, PIECES, run, 0)
    for j in range(peers - 1):
        piece_copy(PIECES - 1, j).wait_send()
        slot_copy(j).wait_send()
    others = pl.ds(0, peers - 1)
    pltpu.make_async_copy(slots_ref.at[others], slots_ref.at[others], slot_recv).wait()
    pltpu.make_async_copy(land_ref.at[others], land_ref.at[others], land_sem).wait()


def finish_kernel(land_ref, slots_ref, stat_ref, out_hbm, mom_ref, ready, out_sem):
    peers, rows, width = land_ref.shape
    tiles = width // LANES
    row = lambda ref, first: jnp.concatenate([ref[pl.ds(first + t, 1)] for t in range(tiles)], axis=1)
    center, variance = row(stat_ref, 0), row(stat_ref, tiles)
    mom_ref[pl.ds(0, 1)] = center
    mom_ref[pl.ds(1, 1)] = variance
    factor = lax.rsqrt(variance + eps_value)
    center = jnp.broadcast_to(center, (8, width))
    factor = jnp.broadcast_to(factor, (8, width))

    def block(s, carry):
        for r in range(0, rows, 8):
            scaled = (land_ref[s, pl.ds(r, 8)] - center) * factor
            ready[s, pl.ds(r, 8)] = jnp.clip(scaled, -clip_value, clip_value)
        pltpu.make_async_copy(ready.at[s], out_hbm.at[slots_ref[s, 0]], out_sem).start()
        return carry

    lax.fori_loop(0, peers, block, 0)
    pltpu.make_async_copy(ready, out_hbm, out_sem).wait()


def body(features, dest, slot):
    row_count, width = features.shape
    peers = lax.axis_size("inner")
    blocks = dest.shape[0]
    rows = row_count // blocks
    tiles = width // LANES
    vmem = pl.BlockSpec(memory_space=pltpu.VMEM)
    hbm = pl.BlockSpec(memory_space=pltpu.HBM)
    smem = pl.BlockSpec(memory_space=pltpu.SMEM)
    operands = (
        dest.reshape(1, blocks),
        slot.reshape(1, blocks),
        features.reshape(blocks, rows, width),
    )
    landed, slots, stats = pl.pallas_call(
        exchange_kernel,
        out_shape=[
            pltpu.VMEM((peers, rows, width), jnp.float32),
            pltpu.VMEM((peers, LANES), jnp.int32),
            pltpu.VMEM((2 * tiles, LANES), jnp.float32),
        ],
        in_specs=[hbm, hbm, hbm],
        out_specs=[vmem, vmem, vmem],
        scratch_shapes=[
            pltpu.VMEM((blocks, rows, width), jnp.float32),
            pltpu.VMEM((peers, rows, width), jnp.float32),
            pltpu.VMEM((1, blocks), jnp.int32),
            pltpu.VMEM((1, blocks), jnp.int32),
            pltpu.VMEM((peers, LANES), jnp.int32),
            pltpu.VMEM((peers, LANES), jnp.int32),
            pltpu.SMEM((peers, LANES), jnp.int32),
            pltpu.VMEM((4, 2 * tiles, LANES), jnp.float32),
            pltpu.VMEM((10, 2 * tiles, LANES), jnp.float32),
            pltpu.SemaphoreType.DMA((LOADS + 3,)),
            pltpu.SemaphoreType.DMA((peers - 1,)),
            pltpu.SemaphoreType.DMA,
            pltpu.SemaphoreType.DMA((peers - 1,)),
            pltpu.SemaphoreType.DMA,
            pltpu.SemaphoreType.DMA((10,)),
            pltpu.SemaphoreType.DMA((10,)),
        ],
        compiler_params=pltpu.CompilerParams(
            collective_id=0, has_side_effects=True, vmem_limit_bytes=48 * 2**20
        ),
    )(*(pltpu.with_memory_space_constraint(a, pltpu.HBM) for a in operands))
    standardized, moments = pl.pallas_call(
        finish_kernel,
        out_shape=[
            jax.ShapeDtypeStruct((peers, rows, width), jnp.float32),
            jax.ShapeDtypeStruct((2, width), jnp.float32),
        ],
        in_specs=[vmem, smem, vmem],
        out_specs=[hbm, vmem],
        scratch_shapes=[
            pltpu.VMEM((peers, rows, width), jnp.float32),
            pltpu.SemaphoreType.DMA,
        ],
        compiler_params=pltpu.CompilerParams(vmem_limit_bytes=24 * 2**20),
    )(landed, slots, stats)
    return (standardized.reshape(row_count, width), moments)


def solution(mesh):
    in_specs = (P(("outer", "inner"), None), P(("outer", "inner")), P(("outer", "inner")))
    out_specs = (P(("outer", "inner"), None), P())
    return jax.shard_map(body, mesh=mesh, in_specs=in_specs, out_specs=out_specs, check_vma=False)
```

time: 134 us -> 111 us (0.83)
  the two profiles are of different devices: /device:TPU:92 before, /device:TPU:1 now
where the time goes in v2:
time: 111 us
  Pallas kernels  110 us (99%)
    pallas_call x1, Pallas kernels, body(): pl.pallas_call(exchange_kernel, out_shape=[pltpu.VMEM((peers, rows, width...  105 us
    pallas_call x1, Pallas kernels, body(): pl.pallas_call(finish_kernel, out_shape=[jax.ShapeDtypeStruct((peers, row...  4.94 us

profile of v2, /device:TPU:1, one launch (start us, length us, event | category | flops | bytes accessed | tf_op | source)
XLA Modules:
  0.0 111.0 jit_solution(5005099983248798981)
XLA Ops:
  0.6 105.5 %shard_map.50 = (f32[64,32,1024]{2,1,0:T(8,128)S(1)}, s32[64,128]{1,0:T(8,128)S(1)}, f32[16,128]{1,0:T(8,128)S(1)}) custom-call(s32[1,64]{1,0:T(1,128)} %bitcast.5, s32[1,64]{1,0:T(1,128)} %bitcast.6, f32[64,32,1024]{2,1,0:T(8,128)} %bitcast.4), custom_call_target="tpu_custom_call" | custom-call | tf_op jit(solution)/shard_map/pallas_call | solution.py:272
  106.1 4.9 %shard_map.51 = (f32[64,32,1024]{2,1,0:T(8,128)}, f32[2,1024]{1,0:T(2,128)}) custom-call(f32[64,32,1024]{2,1,0:T(8,128)S(1)} %get-tuple-element.7.land_ref, s32[64,128]{1,0:T(8,128)S(1)} %get-tuple-element.8.slots_ref, f32[16,128]{1,0:T(8,128)S(1)} %get-tuple-element.9.stat_ref), custom_call_target="tpu_custom_call" | custom-call | tf_op jit(solution)/shard_map/pallas_call | solution.py:303

commit v3 on v2

--- a/solution.py
+++ b/solution.py
@@ -12,12 +12,16 @@
 clip_value = 3.0
 SIDE = 4
 PIECES = 8
-LOADS = 8
+LOADS = 4
 LANES = 128
 
 
 def hops(offset):
     return sum(min(v, SIDE - v) for v in offset)
+
+
+def axes(offset):
+    return sum(v != 0 for v in offset)
 
 
 def send_order():
@@ -32,7 +36,11 @@
                     left.remove(d)
                     group.append(d)
         groups.append(group)
-    return [d for group in sorted(groups, key=lambda g: hops(g[0])) for d in group]
+    return [d for group in sorted(groups, key=lambda g: (axes(g[0]), hops(g[0]))) for d in group]
+
+
+def close_count():
+    return sum(axes(d) == 1 for d in send_order())
 
 
 def merge_pair(a, b, half):
@@ -43,8 +51,8 @@
 def exchange_kernel(
     dest_hbm, slot_hbm, feat_hbm,
     land_ref, slots_ref, stat_ref,
-    feats, stage, dest_v, slot_v, order_v, slots_v, order_s, moment, peer_moment,
-    load_sem, send_sem, land_sem, slot_send, slot_recv, mom_send, mom_recv,
+    feats_0, feats_1, feats_2, feats_3, stage, stage_close, dest_v, slot_v, order_v, slots_v, slots_in, order_s, moment, peer_moment,
+    two_sem, three_sem, load_sem, send_sem, land_sem, slot_send, slot_recv, mom_send, mom_recv,
 ):
     peers, rows, width = land_ref.shape
     tiles = width // LANES
@@ -58,26 +66,40 @@
         return ((y + dy) % SIDE) * SIDE * SIDE + ((x + dx) % SIDE) * SIDE + (z + dz) % SIDE
 
     barrier = pltpu.get_barrier_semaphore()
+    feats = (feats_0, feats_1, feats_2, feats_3)
     load = peers // LOADS
     loads = [
-        pltpu.make_async_copy(
-            feat_hbm.at[pl.ds(k * load, load)], feats.at[pl.ds(k * load, load)], load_sem.at[k]
-        )
-        for k in range(LOADS)
+        [
+            pltpu.make_async_copy(
+                feat_hbm.at[pl.ds(k * load, load), pl.ds(r * 8, 8)],
+                feats[r].at[pl.ds(k * load, load)],
+                load_sem.at[r * LOADS + k],
+            )
+            for k in range(LOADS)
+        ]
+        for r in range(len(feats))
     ]
     small = [
-        pltpu.make_async_copy(dest_hbm, dest_v, load_sem.at[LOADS]),
-        pltpu.make_async_copy(slot_hbm, slot_v, load_sem.at[LOADS + 1]),
+        pltpu.make_async_copy(dest_hbm, dest_v, load_sem.at[4 * LOADS]),
+        pltpu.make_async_copy(slot_hbm, slot_v, load_sem.at[4 * LOADS + 1]),
     ]
-    for copy in small + loads:
+    for copy in small + loads[0]:
         copy.start()
 
-    def greet(k, carry):
-        pl.semaphore_signal(barrier, inc=1, device_id=(core, me ^ k), device_id_type=MESH)
-        return carry
-
-    lax.fori_loop(1, peers, greet, 0)
+    order_of = send_order()
+    targets = [at(d) for d in order_of]
+    close = close_count()
+    planar = sum(axes(d) <= 2 for d in order_of)
+
+    def greet(semaphore):
+        for j in range(close):
+            pl.semaphore_signal(semaphore, inc=1, device_id=(core, targets[j]), device_id_type=MESH)
+
+    greet(barrier)
     pl.semaphore_signal(barrier, inc=1, device_id=(1 - core, me), device_id_type=MESH)
+    for group in loads[1:]:
+        for copy in group:
+            copy.start()
 
     for copy in small:
         copy.wait()
@@ -88,56 +110,42 @@
     slots = jnp.max(jnp.where(hit, slot_v[...], 0), axis=1, keepdims=True)
     order_v[...] = jnp.broadcast_to(order, order_v.shape)
     slots_v[...] = jnp.broadcast_to(slots, slots_v.shape)
-    to_scalar = pltpu.make_async_copy(order_v, order_s, load_sem.at[LOADS + 2])
+    to_scalar = pltpu.make_async_copy(order_v, order_s, load_sem.at[4 * LOADS + 2])
     to_scalar.start()
-    slots_ref[pl.ds(me, 1)] = slots_v[pl.ds(me, 1)]
-
-    zero = jnp.zeros((8, width), jnp.float32)
-    acc = zero
-    for k in range(LOADS):
-        loads[k].wait()
-
-        def total(b, acc):
-            block = feats[b]
-            for r in range(0, rows, 8):
-                acc = acc + block[r : r + 8]
-            return acc
-
-        acc = lax.fori_loop(k * load, (k + 1) * load, total, acc)
-    center = jnp.sum(acc, axis=0, keepdims=True) * (1.0 / (peers * rows))
-    to_scalar.wait()
+    slots_in[pl.ds(me, 1)] = slots_v[pl.ds(me, 1)]
 
     def part(q):
         return pl.ds((q // col_pieces) * 8, 8), pl.ds(pl.multiple_of((q % col_pieces) * cols, cols), cols)
 
-    def arrange(q):
+    def arrange(q, r):
         def one(p, carry):
-            stage[(p,) + part(q)] = feats[(order_s[p, 0],) + part(q)]
+            stage[(p,) + part(q)] = feats[r][order_s[p, 0], :, part(q)[1]]
             return carry
 
         lax.fori_loop(0, peers, one, 0, unroll=8)
-
-    targets = [at(d) for d in send_order()]
 
     def slot_copy(j):
         return pltpu.make_async_remote_copy(
             src_ref=slots_v.at[pl.ds(targets[j], 1)],
-            dst_ref=slots_ref.at[pl.ds(me, 1)],
+            dst_ref=slots_in.at[pl.ds(me, 1)],
             send_sem=slot_send.at[j],
             recv_sem=slot_recv,
             device_id=(core, targets[j]),
             device_id_type=MESH,
         )
 
-    def piece_copy(q, j):
+    def block_copy(j, where):
         return pltpu.make_async_remote_copy(
-            src_ref=stage.at[(targets[j],) + part(q)],
-            dst_ref=land_ref.at[(me,) + part(q)],
+            src_ref=stage_close.at[(j,) + where] if j < close else stage.at[(targets[j],) + where],
+            dst_ref=land_ref.at[(me,) + where],
             send_sem=send_sem.at[j],
             recv_sem=land_sem,
             device_id=(core, targets[j]),
             device_id_type=MESH,
         )
+
+    def piece_copy(q, j):
+        return block_copy(j, part(q))
 
     def read(ref):
         return ref[pl.ds(0, tiles)], ref[pl.ds(tiles, tiles)]
@@ -182,39 +190,64 @@
         else:
             write(stat_ref, (pair[0], pair[1] / (count * 2.0)))
 
-    arrange(0)
-    pl.semaphore_wait(barrier, peers)
-    for j in range(peers - 1):
+    pl.semaphore_wait(barrier, close + 1)
+    greet(two_sem)
+    to_scalar.wait()
+    for r in range(len(feats)):
+        where = pl.ds(r * 8, 8)
+        for copy in loads[r]:
+            copy.wait()
+        for j in range(close):
+            stage_close[j, where] = feats[r][order_s[targets[j], 0]]
+            block_copy(j, (where,)).start()
+        if r == 0:
+            arrange(0, 0)
+    pl.semaphore_wait(two_sem, close)
+    greet(three_sem)
+    for j in range(close, planar):
         piece_copy(0, j).start()
-    arrange(1)
+    pl.semaphore_wait(three_sem, close)
+    for j in range(planar, peers - 1):
+        piece_copy(0, j).start()
+    arrange(1, 1 // col_pieces)
+
+    zero = jnp.zeros((8, width), jnp.float32)
+    acc = zero
+    for feat in feats:
+        acc = lax.fori_loop(0, peers, lambda b, acc: acc + feat[b], acc, unroll=2)
+    center = jnp.sum(acc, axis=0, keepdims=True) * (1.0 / (peers * rows))
     wide = jnp.broadcast_to(center, (8, width))
-
-    def squares(b, acc):
-        block = feats[b]
-        for r in range(0, rows, 8):
-            gap = block[r : r + 8] - wide
-            acc = acc + gap * gap
-        return acc
-
-    spread = jnp.sum(lax.fori_loop(0, peers, squares, zero), axis=0, keepdims=True)
+    acc = zero
+    for feat in feats:
+
+        def squares(b, acc):
+            gap = feat[b] - wide
+            return acc + gap * gap
+
+        acc = lax.fori_loop(0, peers, squares, acc, unroll=2)
+    spread = jnp.sum(acc, axis=0, keepdims=True)
     for t in range(tiles):
         moment[0, pl.ds(t, 1)] = center[:, t * LANES : (t + 1) * LANES]
         moment[0, pl.ds(tiles + t, 1)] = spread[:, t * LANES : (t + 1) * LANES]
     moment_send(0)
-    land_ref[me] = feats[order_s[me, 0]]
+    for r in range(len(feats)):
+        land_ref[me, pl.ds(r * 8, 8)] = feats[r][order_s[me, 0]]
 
     def run(q, carry):
-        for j in range(peers - 1):
+        for j in range(close, peers - 1):
             piece_copy(q - 1, j).wait_send()
             piece_copy(q, j).start()
 
-            @pl.when(q == 1)
+        @pl.when(q == 1)
+        def _():
+            for j in range(peers - 1):
+                slot_copy(j).start()
+
+        for r in range(len(feats)):
+
+            @pl.when((q + 1) // col_pieces == r)
             def _():
-                slot_copy(j).start()
-
-        @pl.when(q < PIECES - 1)
-        def _():
-            arrange(q + 1)
+                arrange(q + 1, r)
 
         for step in range(4):
 
@@ -225,21 +258,27 @@
         return carry
 
     lax.fori_loop(1, PIECES, run, 0)
+    others = pl.ds(0, peers - 1)
+    pltpu.make_async_copy(slots_in.at[others], slots_in.at[others], slot_recv).wait()
+    pltpu.sync_copy(slots_in, slots_ref)
+    for j in range(close):
+        block_copy(j, ()).wait_send()
+    for j in range(close, peers - 1):
+        piece_copy(PIECES - 1, j).wait_send()
     for j in range(peers - 1):
-        piece_copy(PIECES - 1, j).wait_send()
         slot_copy(j).wait_send()
-    others = pl.ds(0, peers - 1)
-    pltpu.make_async_copy(slots_ref.at[others], slots_ref.at[others], slot_recv).wait()
     pltpu.make_async_copy(land_ref.at[others], land_ref.at[others], land_sem).wait()
 
 
-def finish_kernel(land_ref, slots_ref, stat_ref, out_hbm, mom_ref, ready, out_sem):
+def finish_kernel(land_ref, slots_ref, stat_ref, out_hbm, mom_hbm, ready, mom, out_sem, mom_sem):
     peers, rows, width = land_ref.shape
     tiles = width // LANES
     row = lambda ref, first: jnp.concatenate([ref[pl.ds(first + t, 1)] for t in range(tiles)], axis=1)
     center, variance = row(stat_ref, 0), row(stat_ref, tiles)
-    mom_ref[pl.ds(0, 1)] = center
-    mom_ref[pl.ds(1, 1)] = variance
+    mom[pl.ds(0, 1)] = center
+    mom[pl.ds(1, 1)] = variance
+    mom_copy = pltpu.make_async_copy(mom, mom_hbm, mom_sem)
+    mom_copy.start()
     factor = lax.rsqrt(variance + eps_value)
     center = jnp.broadcast_to(center, (8, width))
     factor = jnp.broadcast_to(factor, (8, width))
@@ -252,6 +291,7 @@
         return carry
 
     lax.fori_loop(0, peers, block, 0)
+    mom_copy.wait()
     pltpu.make_async_copy(ready, out_hbm, out_sem).wait()
 
 
@@ -273,22 +313,29 @@
         exchange_kernel,
         out_shape=[
             pltpu.VMEM((peers, rows, width), jnp.float32),
-            pltpu.VMEM((peers, LANES), jnp.int32),
+            pltpu.SMEM((peers, LANES), jnp.int32),
             pltpu.VMEM((2 * tiles, LANES), jnp.float32),
         ],
         in_specs=[hbm, hbm, hbm],
-        out_specs=[vmem, vmem, vmem],
+        out_specs=[vmem, smem, vmem],
         scratch_shapes=[
-            pltpu.VMEM((blocks, rows, width), jnp.float32),
+            pltpu.VMEM((blocks, 8, width), jnp.float32),
+            pltpu.VMEM((blocks, 8, width), jnp.float32),
+            pltpu.VMEM((blocks, 8, width), jnp.float32),
+            pltpu.VMEM((blocks, 8, width), jnp.float32),
             pltpu.VMEM((peers, rows, width), jnp.float32),
+            pltpu.VMEM((close_count(), rows, width), jnp.float32),
             pltpu.VMEM((1, blocks), jnp.int32),
             pltpu.VMEM((1, blocks), jnp.int32),
+            pltpu.VMEM((peers, LANES), jnp.int32),
             pltpu.VMEM((peers, LANES), jnp.int32),
             pltpu.VMEM((peers, LANES), jnp.int32),
             pltpu.SMEM((peers, LANES), jnp.int32),
             pltpu.VMEM((4, 2 * tiles, LANES), jnp.float32),
             pltpu.VMEM((10, 2 * tiles, LANES), jnp.float32),
-            pltpu.SemaphoreType.DMA((LOADS + 3,)),
+            pltpu.SemaphoreType.REGULAR,
+            pltpu.SemaphoreType.REGULAR,
+            pltpu.SemaphoreType.DMA((4 * LOADS + 3,)),
             pltpu.SemaphoreType.DMA((peers - 1,)),
             pltpu.SemaphoreType.DMA,
             pltpu.SemaphoreType.DMA((peers - 1,)),
@@ -307,9 +354,11 @@
             jax.ShapeDtypeStruct((2, width), jnp.float32),
         ],
         in_specs=[vmem, smem, vmem],
-        out_specs=[hbm, vmem],
+        out_specs=[hbm, hbm],
         scratch_shapes=[
             pltpu.VMEM((peers, rows, width), jnp.float32),
+            pltpu.VMEM((2, width), jnp.float32),
+            pltpu.SemaphoreType.DMA,
             pltpu.SemaphoreType.DMA,
         ],
         compiler_params=pltpu.CompilerParams(vmem_limit_bytes=24 * 2**20),

time: 111 us -> 108 us (0.973)
  Pallas kernels: 110 us -> 107 us
    pallas_call x1, Pallas kernels: 4.94 us -> 3.28 us  [body(): pl.pallas_call(finish_kernel, out_shape=[jax.ShapeDtypeStruct((peers, row...]
    pallas_call x1, Pallas kernels: 105 us -> 104 us  [body(): pl.pallas_call(exchange_kernel, out_shape=[pltpu.VMEM((peers, rows, width...]
where the time goes in v3:
time: 108 us
  Pallas kernels  107 us (99%)
    pallas_call x1, Pallas kernels, body(): pl.pallas_call(exchange_kernel, out_shape=[pltpu.VMEM((peers, rows, width...  104 us
    pallas_call x1, Pallas kernels, body(): pl.pallas_call(finish_kernel, out_shape=[jax.ShapeDtypeStruct((peers, row...  3.28 us

profile of v3, /device:TPU:1, one launch (start us, length us, event | category | flops | bytes accessed | tf_op | source)
XLA Modules:
  0.0 107.8 jit_solution(2595718835993971095)
XLA Ops:
  0.6 103.9 %shard_map.50 = (f32[64,32,1024]{2,1,0:T(8,128)S(1)}, s32[64,128]{1,0:T(8,128)S(4)}, f32[16,128]{1,0:T(8,128)S(1)}) custom-call(s32[1,64]{1,0:T(1,128)} %bitcast.5, s32[1,64]{1,0:T(1,128)} %bitcast.6, f32[64,32,1024]{2,1,0:T(8,128)} %bitcast.4), custom_call_target="tpu_custom_call" | custom-call | tf_op jit(solution)/shard_map/pallas_call | solution.py:312
  104.5 3.3 %shard_map.51 = (f32[64,32,1024]{2,1,0:T(8,128)}, f32[2,1024]{1,0:T(2,128)}) custom-call(f32[64,32,1024]{2,1,0:T(8,128)S(1)} %get-tuple-element.7.land_ref, s32[64,128]{1,0:T(8,128)S(4)} %get-tuple-element.8.slots_ref, f32[16,128]{1,0:T(8,128)S(1)} %get-tuple-element.9.stat_ref), custom_call_target="tpu_custom_call" | custom-call | tf_op jit(solution)/shard_map/pallas_call | solution.py:350

commit v4 on v3

--- a/solution.py
+++ b/solution.py
@@ -12,7 +12,7 @@
 clip_value = 3.0
 SIDE = 4
 PIECES = 8
-LOADS = 4
+LOADS = 2
 LANES = 128
 
 
@@ -62,7 +62,7 @@
     y, x, z = me // (SIDE * SIDE), (me // SIDE) % SIDE, me % SIDE
 
     def at(offset):
-        dy, dx, dz = offset
+        dy, dx, dz = (a + core * (b - a) for a, b in zip(offset, offset[1:] + offset[:1]))
         return ((y + dy) % SIDE) * SIDE * SIDE + ((x + dx) % SIDE) * SIDE + (z + dz) % SIDE
 
     barrier = pltpu.get_barrier_semaphore()
@@ -83,9 +83,6 @@
         pltpu.make_async_copy(dest_hbm, dest_v, load_sem.at[4 * LOADS]),
         pltpu.make_async_copy(slot_hbm, slot_v, load_sem.at[4 * LOADS + 1]),
     ]
-    for copy in small + loads[0]:
-        copy.start()
-
     order_of = send_order()
     targets = [at(d) for d in order_of]
     close = close_count()
@@ -97,6 +94,8 @@
 
     greet(barrier)
     pl.semaphore_signal(barrier, inc=1, device_id=(1 - core, me), device_id_type=MESH)
+    for copy in small + loads[0]:
+        copy.start()
     for group in loads[1:]:
         for copy in group:
             copy.start()
@@ -108,10 +107,13 @@
     ids = lax.broadcasted_iota(jnp.int32, (peers, blocks), 1)
     order = jnp.max(jnp.where(hit, ids, 0), axis=1, keepdims=True)
     slots = jnp.max(jnp.where(hit, slot_v[...], 0), axis=1, keepdims=True)
-    order_v[...] = jnp.broadcast_to(order, order_v.shape)
+    same = lax.broadcasted_iota(jnp.int32, (peers, peers), 0) == lax.broadcasted_iota(jnp.int32, (peers, peers), 1)
+    order_v[...] = jnp.max(jnp.where(same, order, 0), axis=0, keepdims=True)
     slots_v[...] = jnp.broadcast_to(slots, slots_v.shape)
     to_scalar = pltpu.make_async_copy(order_v, order_s, load_sem.at[4 * LOADS + 2])
     to_scalar.start()
+    dest_row, ids_row = dest_v[...], lax.broadcasted_iota(jnp.int32, (1, blocks), 1)
+    sources = [jnp.max(jnp.where(dest_row == targets[j], ids_row, 0)) for j in range(close)]
     slots_in[pl.ds(me, 1)] = slots_v[pl.ds(me, 1)]
 
     def part(q):
@@ -119,7 +121,7 @@
 
     def arrange(q, r):
         def one(p, carry):
-            stage[(p,) + part(q)] = feats[r][order_s[p, 0], :, part(q)[1]]
+            stage[(p,) + part(q)] = feats[r][order_s[0, p], :, part(q)[1]]
             return carry
 
         lax.fori_loop(0, peers, one, 0, unroll=8)
@@ -190,17 +192,19 @@
         else:
             write(stat_ref, (pair[0], pair[1] / (count * 2.0)))
 
-    pl.semaphore_wait(barrier, close + 1)
-    greet(two_sem)
-    to_scalar.wait()
     for r in range(len(feats)):
         where = pl.ds(r * 8, 8)
         for copy in loads[r]:
             copy.wait()
         for j in range(close):
-            stage_close[j, where] = feats[r][order_s[targets[j], 0]]
+            stage_close[j, where] = feats[r][sources[j]]
+        if r == 0:
+            pl.semaphore_wait(barrier, close + 1)
+        for j in range(close):
             block_copy(j, (where,)).start()
         if r == 0:
+            greet(two_sem)
+            to_scalar.wait()
             arrange(0, 0)
     pl.semaphore_wait(two_sem, close)
     greet(three_sem)
@@ -231,10 +235,10 @@
         moment[0, pl.ds(tiles + t, 1)] = spread[:, t * LANES : (t + 1) * LANES]
     moment_send(0)
     for r in range(len(feats)):
-        land_ref[me, pl.ds(r * 8, 8)] = feats[r][order_s[me, 0]]
+        land_ref[me, pl.ds(r * 8, 8)] = feats[r][order_s[0, me]]
 
     def run(q, carry):
-        for j in range(close, peers - 1):
+        for j in sorted(range(close, peers - 1), key=lambda j: hops(order_of[j])):
             piece_copy(q - 1, j).wait_send()
             piece_copy(q, j).start()
 
@@ -327,10 +331,10 @@
             pltpu.VMEM((close_count(), rows, width), jnp.float32),
             pltpu.VMEM((1, blocks), jnp.int32),
             pltpu.VMEM((1, blocks), jnp.int32),
+            pltpu.VMEM((1, peers), jnp.int32),
             pltpu.VMEM((peers, LANES), jnp.int32),
             pltpu.VMEM((peers, LANES), jnp.int32),
-            pltpu.VMEM((peers, LANES), jnp.int32),
-            pltpu.SMEM((peers, LANES), jnp.int32),
+            pltpu.SMEM((1, peers), jnp.int32),
             pltpu.VMEM((4, 2 * tiles, LANES), jnp.float32),
             pltpu.VMEM((10, 2 * tiles, LANES), jnp.float32),
             pltpu.SemaphoreType.REGULAR,

time: 108 us -> 108 us (level)
  no operation moved by 1% of the time
where the time goes in v4:
time: 108 us
  Pallas kernels  107 us (99%)
    pallas_call x1, Pallas kernels, body(): pl.pallas_call(exchange_kernel, out_shape=[pltpu.VMEM((peers, rows, width...  104 us
    pallas_call x1, Pallas kernels, body(): pl.pallas_call(finish_kernel, out_shape=[jax.ShapeDtypeStruct((peers, row...  3.28 us

profile of v4, /device:TPU:1, one launch (start us, length us, event | category | flops | bytes accessed | tf_op | source)
XLA Modules:
  0.0 107.6 jit_solution(11657926389715605006)
XLA Ops:
  0.6 103.7 %shard_map.50 = (f32[64,32,1024]{2,1,0:T(8,128)S(1)}, s32[64,128]{1,0:T(8,128)S(4)}, f32[16,128]{1,0:T(8,128)S(1)}) custom-call(s32[1,64]{1,0:T(1,128)} %bitcast.5, s32[1,64]{1,0:T(1,128)} %bitcast.6, f32[64,32,1024]{2,1,0:T(8,128)} %bitcast.4), custom_call_target="tpu_custom_call" | custom-call | tf_op jit(solution)/shard_map/pallas_call | solution.py:316
  104.3 3.3 %shard_map.51 = (f32[64,32,1024]{2,1,0:T(8,128)}, f32[2,1024]{1,0:T(2,128)}) custom-call(f32[64,32,1024]{2,1,0:T(8,128)S(1)} %get-tuple-element.7.land_ref, s32[64,128]{1,0:T(8,128)S(4)} %get-tuple-element.8.slots_ref, f32[16,128]{1,0:T(8,128)S(1)} %get-tuple-element.9.stat_ref), custom_call_target="tpu_custom_call" | custom-call | tf_op jit(solution)/shard_map/pallas_call | solution.py:354
